TPU v7x, 32 devices: a whole 2x2x4 slice. The times are simulated.
32 devices in a mesh: dp: 8 (over z, y), pipe: 2 (over x), tensor: 2 (over core).
Axes of the slice: x: 2, y: 2, z: 4, core: 2. Of those that a mesh axis runs over, the one named last changes fastest.
Arguments:
- hidden: bfloat16 [2, 1024, 8192], P('pipe', 'dp', 'tensor'), may hold values from -6 to 6
- doc_lengths: int32 [2, 8, 8], P('pipe', 'dp'), may hold values from 1 to 32, 128 in all within a row
- doc_target: int32 [2, 8, 8], P('pipe', 'dp'), may hold values from 0 to 7, each once within a row
- norm_gain: float32 [2, 8192], P('pipe'), may hold values from 0.5 to 1.5
- q_weight: bfloat16 [2, 8192, 8192], P('pipe', None, 'tensor'), may hold values from -0.0625 to 0.0625
- kv_weight: bfloat16 [2, 8192, 2048], P('pipe', None, 'tensor'), may hold values from -0.0625 to 0.0625
Outputs:
- balanced: bfloat16 [2, 2048, 8192], P('pipe', 'dp', 'tensor')
Inputs may be any that keep to these rules, and one draw needn't show every extreme that they name: `doc_lengths`: each row of lengths sums to 128 and its largest entry is exactly 32. `doc_target`: each row is a permutation of the dp indices.
All inputs are finite; a program needn't handle non-finite values.
Results may differ from a plain program's by a relative error of at most 0.0067.
Values may be sent and summed in bfloat16 or wider, within the bound.
A program may use at most 128 MiB of HBM per device.

v0:
```python
import jax
import jax.numpy as jnp
from jax import lax
from jax.sharding import PartitionSpec as P

D = 8192
HD = 128
KV_HEADS = 8
STEPS = 2


def passed_along(block, axis, distance):
    devices = range(lax.axis_size(axis))
    route = [((i - distance) % len(devices), i) for i in devices]
    return lax.ppermute(block, axis, route)


def build_send(token_rows, lengths, targets, capacity, groups):
    ordinal = jnp.arange(groups, dtype=jnp.int32)
    offsets = jnp.cumsum(lengths) - lengths
    onehot = (targets[None, :] == ordinal[:, None]).astype(jnp.int32)
    doc_sizes = jnp.sum(onehot * lengths[None, :], axis=1)
    doc_starts = jnp.sum(onehot * offsets[None, :], axis=1)
    within = jnp.arange(capacity, dtype=jnp.int32)
    row_index = jnp.minimum(doc_starts[:, None] + within[None, :], token_rows.shape[0] - 1)
    picked = jnp.take(token_rows, row_index.reshape(-1), axis=0).reshape(
        groups, capacity, token_rows.shape[1]
    )
    inside = within[None, :] < doc_sizes[:, None]
    return (jnp.where(inside[:, :, None], picked, jnp.zeros_like(picked)), doc_sizes)


def doc_masks(lengths, length):
    within = jnp.arange(length, dtype=jnp.int32)
    doc_ends = jnp.cumsum(lengths)
    segment = jnp.sum((within[:, None] >= doc_ends[None, :]).astype(jnp.int32), axis=1)
    causal = within[:, None] >= within[None, :]
    return (segment[:, None] == segment[None, :]) & causal


def attend_heads(queries, kv_local, allowed, local_rank):
    row_count = queries.shape[0]
    local_heads = queries.shape[1] // HD
    per_group = D // HD // KV_HEADS
    kv_count = max(1, local_heads // per_group)
    kv_first = local_rank * local_heads // per_group
    kv_whole = lax.all_gather(kv_local, "tensor", axis=1, tiled=True)
    kv_heads = kv_whole.reshape(row_count, 2, HD, KV_HEADS)
    own_heads = lax.dynamic_slice_in_dim(kv_heads, kv_first, kv_count, 3)
    key_rows = own_heads[:, 0]
    values = own_heads[:, 1]
    grouped = queries.reshape(row_count, kv_count, local_heads // kv_count, HD)
    scores = jnp.einsum(
        "qcph,khc->cpqk", grouped, key_rows, preferred_element_type=jnp.float32
    ) * HD ** (-0.5)
    exp_scores = jnp.where(allowed[None, None], jnp.exp(scores), 0.0)
    probabilities = (exp_scores / jnp.sum(exp_scores, axis=-1, keepdims=True)).astype(jnp.bfloat16)
    attended = jnp.einsum(
        "cpqk,khc->qcph", probabilities, values, preferred_element_type=jnp.float32
    )
    return attended.reshape(row_count, queries.shape[1])


def layer_pass(current, gain_full, query_cols, kv_cols, allowed):
    local_rank = lax.axis_index("tensor")
    widened = current.astype(jnp.float32)
    whole = lax.all_gather(current, "tensor", axis=1, tiled=True)
    whole_wide = whole.astype(jnp.float32)
    scale_row = lax.rsqrt(jnp.sum(whole_wide * whole_wide, axis=-1) / D + 1e-05)
    normed_full = (whole_wide * scale_row[:, None] * gain_full).astype(jnp.bfloat16)
    query_sum = jnp.dot(normed_full, query_cols, preferred_element_type=jnp.float32)
    kv_sum = jnp.dot(normed_full, kv_cols, preferred_element_type=jnp.float32)
    queries = query_sum.astype(jnp.bfloat16)
    kv_local = kv_sum.astype(jnp.bfloat16)
    attended = attend_heads(queries, kv_local, allowed, local_rank)
    return (widened + attended).astype(jnp.bfloat16)


def on_device(hidden, doc_lengths, doc_target, norm_gain, q_weight, kv_weight):
    groups = lax.axis_size("dp")
    current = hidden[0]
    lengths = doc_lengths[0, 0]
    targets = doc_target[0, 0]
    capacity = current.shape[0] // 4
    gain_full = norm_gain[0]
    query_cols = q_weight[0]
    kv_cols = kv_weight[0]
    carried = jnp.stack([lengths, targets]).astype(jnp.bfloat16)
    for layer_step in range(STEPS):
        allowed = doc_masks(carried[0].astype(jnp.int32), current.shape[0])
        current = layer_pass(current, gain_full, query_cols, kv_cols, allowed)
        if layer_step + 1 < STEPS:
            current, carried = passed_along((current, carried), "pipe", 1)
    final_lengths = carried[0].astype(jnp.int32)
    final_targets = carried[1].astype(jnp.int32)
    packed, doc_sizes = build_send(current, final_lengths, final_targets, capacity, groups)
    received = lax.all_to_all(packed, "dp", split_axis=0, concat_axis=0, tiled=True)
    return received.reshape(1, groups * capacity, received.shape[2])


def solution(mesh):
    placed = (
        P("pipe", "dp", "tensor"),
        P("pipe", "dp", None),
        P("pipe", "dp", None),
        P("pipe", None),
        P("pipe", None, "tensor"),
        P("pipe", None, "tensor"),
    )
    return jax.shard_map(
        on_device, mesh=mesh, in_specs=placed, out_specs=P("pipe", "dp", "tensor"), check_vma=False
    )
```

profile of v0, /device:TPU:0, one launch (start us, length us, event | category | flops | bytes accessed | tf_op | source)
XLA Modules:
  0.0 209.5 jit_solution(3206547490324969738)
XLA Ops:
  6.5 0.7 all-gather.6.cloned.1.call-update
  7.3 0.7 convert_bitcast_fusion.3
  8.0 0.2 reduce-window.14
  8.2 0.1 convert_reduce_fusion.1
  8.3 0.1 fusion.52
  8.4 13.8 %all-gather.6.cloned.1.call-done = bf16[1,128,8192]{2,1,0:T(8,128)(2,1)} async-done(((bf16[1,128,4096]{2,1,0:T(8,128)(2,1)}), bf16[1,128,8192]{2,1,0:T(8,128)(2,1)}) %all-gather.6.cloned.1.call-update) | async-done | bytes 2097168 | tf_op jit(solution)/shard_map/all_gather | solution.py:67
  22.2 2.2 %fusion.17 = f32[128]{0:T(128)S(1)} fusion(bf16[1,128,8192]{2,1,0:T(8,128)(2,1)} %all-gather.6.cloned.1.call-done), kind=kLoop, calls=%fused_computation.18 | loop fusion | flops 3145600 | bytes 2097664 | tf_op jit(solution)/shard_map/reduce_sum | solution.py:69
  24.5 8.1 %fusion.29 = bf16[128,1024]{1,0:T(8,128)(2,1)S(1)} fusion(bf16[1,8192,1024]{2,1,0:T(8,128)(2,1)} %param.11, bf16[1,128,8192]{2,1,0:T(8,128)(2,1)S(1)} %copy-done, f32[8192]{0:T(1024)S(1)} %bitcast.125, f32[128]{0:T(128)S(1)} %add_rsqrt_fusion.1), kind=kOutput, calls=%fused_computation.33 | convolution fusion | flops 2151809024 | bytes 19169792 | tf_op jit(solution)/shard_map/dot_general | solution.py:72
  32.6 2.2 %all_gather.13 = bf16[128,2048]{1,0:T(8,128)(2,1)S(1)} all-gather(bf16[128,1024]{1,0:T(8,128)(2,1)S(1)} %fusion.29), channel_id=1, replica_groups=mesh['dp'=8,'pipe'=2,'tensor'=2] {'tensor'}, dimensions={1}, use_global_device_ids=true | all-gather | bytes 786432 | tf_op jit(solution)/shard_map/all_gather | solution.py:47
  34.8 0.3 copy.29
  35.1 0.1 constant_dynamic-slice_fusion
  35.2 0.1 copy.53
  35.4 23.0 %fusion.26 = bf16[16,8,32,128]{3,1,2,0:T(8,128)(2,1)S(1)} fusion(bf16[1,8192,4096]{2,1,0:T(8,128)(2,1)} %param.10, bf16[1,128,8192]{2,1,0:T(8,128)(2,1)S(1)} %copy-done, f32[8192]{0:T(1024)S(1)} %bitcast.126, f32[128]{0:T(128)S(1)} %add_rsqrt_fusion.1), kind=kOutput, calls=%fused_computation.32 | convolution fusion | flops 8594653184 | bytes 70287872 | tf_op jit(solution)/shard_map/dot_general | solution.py:71
  58.4 0.2 copy.57
  58.6 0.1 copy.52
  58.7 0.8 fusion.21
  59.6 1.9 fusion.39
  61.5 2.0 copy.34
  63.5 0.2 fusion.20
  63.7 1.8 collective-permute-start.1
  65.5 23.6 %collective-permute-done.1 = bf16[128,4096]{1,0:T(8,128)(2,1)S(1)} collective-permute-done((bf16[128,4096]{1,0:T(8,128)(2,1)S(1)}, bf16[128,4096]{1,0:T(8,128)(2,1)S(1)}, u32[]{:S(2)}, u32[]{:S(2)}) %collective-permute-start.1) | collective-permute-done | bytes 1048608 | tf_op jit(solution)/shard_map/ppermute | solution.py:15
  89.2 1.0 copy-done.3
  90.2 1.8 collective-permute-start
  92.0 1.8 collective-permute-done
  93.8 0.2 reduce-window.13
  94.0 0.1 select_reduce_fusion.1
  94.2 0.1 min.22
  94.3 0.1 convert_reduce_fusion
  94.4 0.1 compare_and_fusion
  94.6 0.1 fusion.51
  94.7 7.4 %all-gather.4.cloned.1.call-done = bf16[128,8192]{1,0:T(8,128)(2,1)} async-done(((bf16[128,4096]{1,0:T(8,128)(2,1)}), bf16[128,8192]{1,0:T(8,128)(2,1)}) %all-gather.4.cloned.1.call-update) | async-done | bytes 2097168 | tf_op jit(solution)/shard_map/all_gather | solution.py:67
  102.1 2.2 %fusion.14 = f32[128]{0:T(128)S(1)} fusion(bf16[128,8192]{1,0:T(8,128)(2,1)} %all-gather.4.cloned.1.call-done), kind=kLoop, calls=%fused_computation.15 | loop fusion | flops 3145600 | bytes 2097664 | tf_op jit(solution)/shard_map/reduce_sum | solution.py:69
  104.3 8.1 %fusion.32 = bf16[128,1024]{1,0:T(8,128)(2,1)S(1)} fusion(bf16[1,8192,1024]{2,1,0:T(8,128)(2,1)} %param.11, bf16[128,8192]{1,0:T(8,128)(2,1)S(1)} %copy-done.1, f32[128]{0:T(128)S(1)} %add_rsqrt_fusion, f32[8192]{0:T(1024)S(1)} %bitcast.127), kind=kOutput, calls=%fused_computation.34 | convolution fusion | flops 2151809024 | bytes 19169792 | tf_op jit(solution)/shard_map/dot_general | solution.py:72
  112.5 2.4 %all_gather.15 = bf16[128,2048]{1,0:T(8,128)(2,1)S(1)} all-gather(bf16[128,1024]{1,0:T(8,128)(2,1)S(1)} %fusion.32), channel_id=1, replica_groups=mesh['dp'=8,'pipe'=2,'tensor'=2] {'tensor'}, dimensions={1}, use_global_device_ids=true | all-gather | bytes 786432 | tf_op jit(solution)/shard_map/all_gather | solution.py:47
  114.8 0.3 copy.35
  115.1 0.1 constant_dynamic-slice_fusion.3
  115.3 0.1 copy.56
  115.4 23.0 %fusion.23 = bf16[16,8,32,128]{3,1,2,0:T(8,128)(2,1)S(1)} fusion(bf16[1,8192,4096]{2,1,0:T(8,128)(2,1)} %param.10, bf16[128,8192]{1,0:T(8,128)(2,1)S(1)} %copy-done.1, f32[128]{0:T(128)S(1)} %add_rsqrt_fusion, f32[8192]{0:T(1024)S(1)} %bitcast.128), kind=kOutput, calls=%fused_computation.31 | convolution fusion | flops 8594653184 | bytes 70287872 | tf_op jit(solution)/shard_map/dot_general | solution.py:71
  138.4 0.2 copy.58
  138.6 0.1 copy.55
  138.8 0.8 fusion.22
  139.6 1.9 fusion.40
  141.5 1.9 copy.40
  143.5 1.4 add_convert_fusion
  144.9 1.8 gather_fusion
  146.8 0.3 select_select_fusion
  147.1 54.2 %all_to_all.5 = bf16[8,32,4096]{2,1,0:T(8,128)(2,1)S(1)} all-to-all(bf16[8,32,4096]{2,1,0:T(8,128)(2,1)S(1)} %select_select_fusion), channel_id=1, replica_groups=mesh['dp'=8,'pipe'=2,'tensor'=2] {'dp'}, dimensions={0} | all-to-all | bytes 4194304 | tf_op jit(solution)/shard_map/all_to_all | solution.py:97
  201.3 1.3 copy.68
  (21 shorter events, 0.3 us)
Async XLA Ops:
  6.5 17.9 %copy-start.4 = (f32[1,8192]{1,0:T(1,128)S(1)}, f32[1,8192]{1,0:T(1,128)}, u32[]{:S(2)}) copy-start(f32[1,8192]{1,0:T(1,128)} %param.9) | copy-start | bytes 98308
  6.5 15.7 %all-gather.6.cloned.1.call-start = ((), (), s32[]{:S(2)}) async-start(), calls=%async_computation.2 | async-start | bytes 3145728 | tf_op jit(solution)/shard_map/all_gather | solution.py:67
  7.3 94.8 %all-gather.4.cloned.1.call-start = ((), (), s32[]{:S(2)}) async-start(), calls=%async_computation.1 | async-start | bytes 3145728 | tf_op jit(solution)/shard_map/all_gather | solution.py:67
  22.2 2.3 %copy-start = (bf16[1,128,8192]{2,1,0:T(8,128)(2,1)S(1)}, bf16[1,128,8192]{2,1,0:T(8,128)(2,1)}, u32[]{:S(2)}) copy-start(bf16[1,128,8192]{2,1,0:T(8,128)(2,1)} %all-gather.6.cloned.1.call-done) | copy-start | bytes 6291460
  61.5 2.0 copy-start.2
  63.7 25.4 %collective-permute-start.1 = (bf16[128,4096]{1,0:T(8,128)(2,1)S(1)}, bf16[128,4096]{1,0:T(8,128)(2,1)S(1)}, u32[]{:S(2)}, u32[]{:S(2)}) collective-permute-start(bf16[128,4096]{1,0:T(8,128)(2,1)S(1)} %fusion.20), channel_id=1, source_target_pairs={{2,0},{0,2},{3,1},{1,3},{6,4},{4,6},{7,5},{5,7},{10,8},{8,10},{11,... | collective-permute-start | bytes 3145736 | tf_op jit(solution)/shard_map/ppermute | solution.py:15
  89.2 1.0 copy-start.3
  90.2 3.6 %collective-permute-start = (bf16[2,8]{1,0:T(2,128)(2,1)S(1)}, bf16[2,8]{1,0:T(2,128)(2,1)S(1)}, u32[]{:S(2)}, u32[]{:S(2)}) collective-permute-start(bf16[2,8]{1,0:T(2,128)(2,1)S(1)} %pad_maximum_fusion), channel_id=1, source_target_pairs={{2,0},{0,2},{3,1},{1,3},{6,4},{4,6},{7,5},{5,7},{10,8},{8,10},{11,... | collective-permute-start | bytes 104 | tf_op jit(solution)/shard_map/ppermute | solution.py:15
  102.1 2.2 %copy-start.1 = (bf16[128,8192]{1,0:T(8,128)(2,1)S(1)}, bf16[128,8192]{1,0:T(8,128)(2,1)}, u32[]{:S(2)}) copy-start(bf16[128,8192]{1,0:T(8,128)(2,1)} %all-gather.4.cloned.1.call-done) | copy-start | bytes 6291460
Sparse Core Ops, SparseCore 0:
  8.9 13.2 all-gather.5
  90.3 11.7 all-gather.3
where the time goes:
time: 210 us; the launch traced here: 209 us
  matrix products  67.7 us (32%)
  blocking collectives  58.8 us (28%)
  waiting for transfers between devices  47.4 us (23%)
  between operations  13.6 us (6%)
  local copies, waits for them, and re-layouts  10 us (5%)
  other arithmetic  8.25 us (4%)
  starting transfers between devices  3.65 us (2%)
    all_to_all x1, blocking collectives, on_device(): lax.all_to_all(packed, 'dp', split_axis=0, concat_axis=0, tiled=True)  54.2 us
    dot_general x2, matrix products, layer_pass(): jnp.dot(normed_full, query_cols, preferred_element_type=jnp.float32)  45.9 us
    ppermute x2, waiting for transfers between devices, passed_along(): return lax.ppermute(block, axis, route)  25.4 us
    all_gather x2, waiting for transfers between devices, layer_pass(): whole = lax.all_gather(current, 'tensor', axis=1, tiled=True)  21.2 us
    dot_general x2, matrix products, layer_pass(): kv_sum = jnp.dot(normed_full, kv_cols, preferred_element_type=jnp.float32)  16.3 us
    all_gather x2, blocking collectives, attend_heads(): kv_whole = lax.all_gather(kv_local, 'tensor', axis=1, tiled=True)  4.54 us
    reduce_sum x2, other arithmetic, layer_pass(): scale_row = lax.rsqrt(jnp.sum(whole_wide * whole_wide, axis=-1) / D + 1e-05)  4.45 us
  transfers between devices with their start and end apart: 4, of which 4 were waited for; matrix products, arithmetic and copies ran while one was open for 1% of the time, Pallas kernels for 0%

commit v1 on v0

--- a/solution.py
+++ b/solution.py
@@ -1,6 +1,10 @@
+import functools
+
 import jax
 import jax.numpy as jnp
 from jax import lax
+from jax.experimental import pallas as pl
+from jax.experimental.pallas import tpu as pltpu
 from jax.sharding import PartitionSpec as P
 
 D = 8192
@@ -98,6 +102,358 @@
     return received.reshape(1, groups * capacity, received.shape[2])
 
 
+CHUNK = 256
+SLOTS = 6
+
+
+def fused_kernel(
+    sizes, hidden, meta, gain, wq, wkv, out,
+    x_own, x_other, h_send, next_own, next_other, meta_next, normed, spread, kv_cols,
+    kv_send, kv_heads, kv_weights, ring, mask, chooser, q_held, packed,
+    sem_x, sem_xs, sem_xr, sem_ms, sem_mr, sem_kvw, sem_ring, sem_kvs, sem_kvr,
+    sem_hs, sem_hr, sem_fs, sem_fr, sem_as, sem_ar, sem_own,
+):
+    n_dp, n_pipe, docs = sizes
+    rows, width = hidden.shape
+    features = gain.shape[1]
+    n_chunks = width // CHUNK
+    kv_chunks = wkv.shape[1] // CHUNK
+    own_kv = kv_heads.shape[2]
+    chunk_heads = CHUNK // HD
+    group_chunks = n_chunks // own_kv
+    capacity = packed.shape[1]
+    dp = lax.axis_index("dp")
+    pipe = lax.axis_index("pipe")
+    side = lax.axis_index("tensor")
+    other = 1 - side
+    following = lax.rem(pipe + 1, n_pipe)
+    preceding = lax.rem(pipe + n_pipe - 1, n_pipe)
+    total = STEPS * n_chunks
+
+    def cols(j):
+        return pl.ds(pl.multiple_of(j * CHUNK, CHUNK), CHUNK)
+
+    def kv_copy(n):
+        return pltpu.make_async_copy(wkv.at[:, cols(n)], kv_weights.at[n], sem_kvw.at[n])
+
+    def ring_copy(c):
+        slot = lax.rem(c, SLOTS)
+        return pltpu.make_async_copy(
+            wq.at[:, cols(lax.rem(c, n_chunks))], ring.at[slot], sem_ring.at[slot]
+        )
+
+    def x_copy(j):
+        return pltpu.make_async_copy(hidden.at[:, cols(j)], x_own.at[j], sem_x.at[j])
+
+    def x_remote(j):
+        return pltpu.make_async_remote_copy(
+            hidden.at[:, cols(j)], x_other.at[j], sem_xs.at[j], sem_xr.at[j],
+            device_id={"tensor": other}, device_id_type=pl.DeviceIdType.MESH,
+        )
+
+    def meta_remote():
+        return pltpu.make_async_remote_copy(
+            meta, meta_next, sem_ms, sem_mr,
+            device_id={"pipe": following}, device_id_type=pl.DeviceIdType.MESH,
+        )
+
+    def kv_remote(layer):
+        return pltpu.make_async_remote_copy(
+            kv_send.at[layer], kv_heads.at[layer, side], sem_kvs.at[layer], sem_kvr.at[layer],
+            device_id={"tensor": other}, device_id_type=pl.DeviceIdType.MESH,
+        )
+
+    def h_remote(j):
+        return pltpu.make_async_remote_copy(
+            h_send.at[j], next_own.at[j], sem_hs.at[j], sem_hr.at[j],
+            device_id={"pipe": following}, device_id_type=pl.DeviceIdType.MESH,
+        )
+
+    def forward_remote(j):
+        return pltpu.make_async_remote_copy(
+            next_own.at[j], next_other.at[j], sem_fs.at[j], sem_fr.at[j],
+            device_id={"tensor": other}, device_id_type=pl.DeviceIdType.MESH,
+        )
+
+    def doc_rows(index):
+        return pl.ds(pl.multiple_of(index * capacity, capacity), capacity)
+
+    def doc_remote(away, j):
+        target = lax.rem(dp + away, n_dp)
+        return pltpu.make_async_remote_copy(
+            packed.at[target, :, cols(j)], out.at[doc_rows(dp), cols(j)],
+            sem_as.at[away], sem_ar.at[away],
+            device_id={"dp": target}, device_id_type=pl.DeviceIdType.MESH,
+        )
+
+    def doc_all(away):
+        target = lax.rem(dp + away, n_dp)
+        source = lax.rem(dp + n_dp - away, n_dp)
+        return pltpu.make_async_remote_copy(
+            packed.at[target], out.at[doc_rows(source)],
+            sem_as.at[away], sem_ar.at[away],
+            device_id={"dp": target}, device_id_type=pl.DeviceIdType.MESH,
+        )
+
+    for j in range(n_chunks):
+        x_copy(j).start()
+    for n in range(kv_chunks):
+        kv_copy(n).start()
+    for c in range(SLOTS):
+        ring_copy(c).start()
+
+    barrier = pltpu.get_barrier_semaphore()
+    pl.semaphore_signal(
+        barrier, inc=1, device_id={"tensor": other}, device_id_type=pl.DeviceIdType.MESH
+    )
+    pl.semaphore_signal(
+        barrier, inc=1, device_id={"pipe": following}, device_id_type=pl.DeviceIdType.MESH
+    )
+    greeted = n_dp + 1
+    if n_pipe > 2:
+        pl.semaphore_signal(
+            barrier, inc=1, device_id={"pipe": preceding}, device_id_type=pl.DeviceIdType.MESH
+        )
+        greeted += 1
+    for away in range(1, n_dp):
+        pl.semaphore_signal(
+            barrier, inc=1, device_id={"dp": lax.rem(dp + away, n_dp)},
+            device_id_type=pl.DeviceIdType.MESH,
+        )
+    pl.semaphore_wait(barrier, greeted)
+    for j in range(n_chunks):
+        x_remote(j).start()
+    meta_remote().start()
+
+    n_kv = kv_cols.shape[1]
+    cols_wide = spread.shape[0]
+    out_col = lax.broadcasted_iota(jnp.int32, (128, n_kv), 1)
+    wanted = lax.rem(out_col, HD) * KV_HEADS + out_col // HD
+
+    def fill_spread(i, carry):
+        base = pl.multiple_of(i * 128, 128)
+        row = lax.broadcasted_iota(jnp.int32, (128, n_kv), 0) + base
+        spread[pl.ds(base, 128), :] = (row == wanted).astype(jnp.float32).astype(jnp.bfloat16)
+        return carry
+
+    lax.fori_loop(0, cols_wide // 128, fill_spread, 0)
+
+    def fill_mask(source):
+        row = lax.broadcasted_iota(jnp.int32, (rows, rows), 0)
+        col = lax.broadcasted_iota(jnp.int32, (rows, rows), 1)
+        row_doc = jnp.zeros((rows, rows), jnp.int32)
+        col_doc = jnp.zeros((rows, rows), jnp.int32)
+        end = jnp.zeros((1, 1), jnp.int32)
+        for d in range(docs):
+            end = end + source[0:1, d:d + 1]
+            row_doc = row_doc + (row >= end).astype(jnp.int32)
+            col_doc = col_doc + (col >= end).astype(jnp.int32)
+        allowed = jnp.where((row_doc == col_doc) & (row >= col), 1.0, 0.0)
+        for i in range(chunk_heads):
+            mask[i * rows:(i + 1) * rows, :] = allowed
+
+    def fill_chooser(source):
+        row = lax.broadcasted_iota(jnp.int32, (1, rows), 1)
+        goal = jnp.full((1, rows), -1, jnp.int32)
+        begin = jnp.zeros((1, 1), jnp.int32)
+        for d in range(docs):
+            end = begin + source[0:1, d:d + 1]
+            place = source[1:2, d:d + 1] * capacity + row - begin
+            goal = jnp.where((row >= begin) & (row < end), place, goal)
+            begin = end
+        slot = lax.broadcasted_iota(jnp.int32, (n_dp * capacity, rows), 0)
+        chooser[...] = (slot == goal).astype(jnp.float32).astype(jnp.bfloat16)
+
+    def normalise(mine, theirs):
+        def squares(j, acc):
+            a = mine[j].astype(jnp.float32)
+            b = theirs[j].astype(jnp.float32)
+            return acc + a * a + b * b
+
+        acc = lax.fori_loop(0, n_chunks, squares, jnp.zeros((rows, CHUNK), jnp.float32))
+        scale = lax.rsqrt(jnp.sum(acc, axis=-1, keepdims=True) / features + 1e-05)
+
+        def write(j, carry):
+            for held, half in ((mine, side), (theirs, other)):
+                where = cols(half * n_chunks + j)
+                wide = held[j].astype(jnp.float32) * scale * gain[:, where]
+                normed[:, where] = wide.astype(jnp.bfloat16)
+            return carry
+
+        lax.fori_loop(0, n_chunks, write, 0)
+
+    def keys_values(layer):
+        def one(n, carry):
+            if layer == 0:
+                kv_copy(n).wait()
+            kv_cols[:, cols(n)] = jnp.dot(
+                normed[...], kv_weights[n], preferred_element_type=jnp.float32
+            ).astype(jnp.bfloat16)
+            return carry
+
+        lax.fori_loop(0, kv_chunks, one, 0)
+        for which, keep in ((other, False), (side, True)):
+            first = pl.multiple_of(which * own_kv * HD, own_kv * HD)
+            heads = jnp.dot(
+                kv_cols[...], spread[:, pl.ds(first, own_kv * HD)],
+                preferred_element_type=jnp.float32,
+            ).astype(jnp.bfloat16)
+            for g in range(own_kv):
+                if keep:
+                    kv_heads[layer, side, g] = heads[:, g * HD:(g + 1) * HD]
+                else:
+                    kv_send[layer, g] = heads[:, g * HD:(g + 1) * HD]
+            if not keep:
+                kv_remote(layer).start()
+
+    def query(c):
+        return jnp.dot(
+            normed[...], ring[lax.rem(c, SLOTS)], preferred_element_type=jnp.float32
+        ).astype(jnp.bfloat16)
+
+    def attend(layer, j, mine):
+        q = q_held[lax.rem(j, 2)]
+        g = j // group_chunks
+        stacked = jnp.concatenate([q[:, i * HD:(i + 1) * HD] for i in range(chunk_heads)], axis=0)
+        scores = lax.dot_general(
+            stacked, kv_heads[layer, 0, g], (((1,), (1,)), ((), ())),
+            preferred_element_type=jnp.float32,
+        ) * HD ** (-0.5)
+        e = jnp.where(mask[...] > 0.0, jnp.exp(scores), 0.0)
+        p = (e * (1.0 / jnp.sum(e, axis=-1, keepdims=True))).astype(jnp.bfloat16)
+        a = jnp.dot(p, kv_heads[layer, 1, g], preferred_element_type=jnp.float32)
+        side_by_side = jnp.concatenate(
+            [a[i * rows:(i + 1) * rows] for i in range(chunk_heads)], axis=1
+        )
+        return (mine[j].astype(jnp.float32) + side_by_side).astype(jnp.bfloat16)
+
+    def refill(c):
+        @pl.when(c + SLOTS < total)
+        def _():
+            ring_copy(c + SLOTS).start()
+
+    def run_layer(layer, mine, finish):
+        base = layer * n_chunks
+        ring_copy(base).wait()
+        q_held[0] = query(base)
+        refill(jnp.int32(base))
+        kv_remote(layer).wait()
+
+        def one(j, carry):
+            c = base + j
+            ring_copy(c).wait()
+            fresh = query(c)
+            done = attend(layer, j - 1, mine)
+            q_held[lax.rem(j, 2)] = fresh
+            refill(c)
+            finish(j - 1, done)
+            return carry
+
+        lax.fori_loop(1, n_chunks, one, 0)
+        finish(n_chunks - 1, attend(layer, n_chunks - 1, mine))
+
+    lag = 4
+
+    def pass_on(j):
+        h_remote(j).wait_recv()
+        forward_remote(j).start()
+
+    def send_next(j, done):
+        h_send[j] = done
+        h_remote(j).start()
+
+        @pl.when(j >= lag)
+        def _():
+            pass_on(j - lag)
+
+    def send_docs(j, done):
+        picked = jnp.dot(chooser[...], done, preferred_element_type=jnp.float32)
+        picked = picked.astype(jnp.bfloat16)
+        for i in range(n_dp):
+            packed[i, :, cols(j)] = picked[i * capacity:(i + 1) * capacity]
+        for away in range(1, n_dp):
+            doc_remote(away, j).start()
+
+    fill_mask(meta)
+    for j in range(n_chunks):
+        x_copy(j).wait()
+    for j in range(n_chunks):
+        x_remote(j).wait()
+    normalise(x_own, x_other)
+    keys_values(0)
+    run_layer(0, x_own, send_next)
+    for j in range(n_chunks - lag, n_chunks):
+        pass_on(j)
+    meta_remote().wait()
+    fill_mask(meta_next)
+    fill_chooser(meta_next)
+    for j in range(n_chunks):
+        forward_remote(j).wait()
+    normalise(next_own, next_other)
+    keys_values(1)
+    run_layer(1, next_own, send_docs)
+    mine = pltpu.make_async_copy(packed.at[dp], out.at[doc_rows(dp)], sem_own)
+    mine.start()
+    for j in range(n_chunks):
+        h_remote(j).wait_send()
+    mine.wait()
+    for away in range(1, n_dp):
+        doc_all(away).wait()
+
+
+def fused_device(sizes, hidden, doc_lengths, doc_target, norm_gain, q_weight, kv_weight):
+    n_dp, n_pipe, docs = sizes
+    rows, width = hidden.shape[1:]
+    features = norm_gain.shape[1]
+    n_chunks = width // CHUNK
+    n_kv = kv_weight.shape[2]
+    kv_chunks = n_kv // CHUNK
+    own_kv = KV_HEADS // 2
+    capacity = rows // 4
+    chunk_heads = CHUNK // HD
+    meta = jnp.zeros((8, 128), jnp.int32)
+    meta = meta.at[0, :docs].set(doc_lengths[0, 0]).at[1, :docs].set(doc_target[0, 0])
+    bf16 = jnp.bfloat16
+    dma = pltpu.SemaphoreType.DMA
+    vmem = pltpu.VMEM
+    blocks = vmem((n_chunks, rows, CHUNK), bf16)
+    result = pl.pallas_call(
+        functools.partial(fused_kernel, sizes),
+        out_shape=jax.ShapeDtypeStruct((n_dp * capacity, width), bf16),
+        in_specs=[
+            pl.BlockSpec(memory_space=pl.ANY),
+            pl.BlockSpec(memory_space=pltpu.VMEM),
+            pl.BlockSpec(memory_space=pltpu.VMEM),
+            pl.BlockSpec(memory_space=pl.ANY),
+            pl.BlockSpec(memory_space=pl.ANY),
+        ],
+        out_specs=pl.BlockSpec(memory_space=pl.ANY),
+        scratch_shapes=[
+            blocks, blocks, blocks, blocks, blocks,
+            vmem((8, 128), jnp.int32),
+            vmem((rows, features), bf16),
+            vmem((n_kv, n_kv), bf16),
+            vmem((rows, n_kv), bf16),
+            vmem((STEPS, own_kv, rows, HD), bf16),
+            vmem((STEPS, 2, own_kv, rows, HD), bf16),
+            vmem((kv_chunks, features, CHUNK), bf16),
+            vmem((SLOTS, features, CHUNK), bf16),
+            vmem((chunk_heads * rows, rows), jnp.float32),
+            vmem((n_dp * capacity, rows), bf16),
+            vmem((2, rows, CHUNK), bf16),
+            vmem((n_dp, capacity, width), bf16),
+            dma((n_chunks,)), dma((n_chunks,)), dma((n_chunks,)), dma, dma,
+            dma((kv_chunks,)), dma((SLOTS,)), dma((STEPS,)), dma((STEPS,)),
+            dma((n_chunks,)), dma((n_chunks,)), dma((n_chunks,)), dma((n_chunks,)),
+            dma((n_dp,)), dma((n_dp,)), dma,
+        ],
+        compiler_params=pltpu.CompilerParams(
+            collective_id=0, has_side_effects=True, vmem_limit_bytes=66 * 1024 * 1000
+        ),
+    )(hidden[0], meta, norm_gain, q_weight[0], kv_weight[0])
+    return result[None]
+
+
 def solution(mesh):
     placed = (
         P("pipe", "dp", "tensor"),
@@ -107,6 +463,10 @@
         P("pipe", None, "tensor"),
         P("pipe", None, "tensor"),
     )
+    run = on_device
+    if mesh.shape["tensor"] == 2:
+        sizes = (mesh.shape["dp"], mesh.shape["pipe"], mesh.shape["dp"])
+        run = functools.partial(fused_device, sizes)
     return jax.shard_map(
-        on_device, mesh=mesh, in_specs=placed, out_specs=P("pipe", "dp", "tensor"), check_vma=False
-    )
+        run, mesh=mesh, in_specs=placed, out_specs=P("pipe", "dp", "tensor"), check_vma=False
+    )

time: 210 us -> 110 us (0.52)
  Pallas kernels: 0 us -> 104 us
  matrix products: 67.7 us -> 0 us
  blocking collectives: 58.8 us -> 0 us
  waiting for transfers between devices: 47.4 us -> 0 us
  between operations: 13.6 us -> 0.01 us
  other arithmetic: 8.25 us -> 0 us
  local copies, waits for them, and re-layouts: 10 us -> 5.68 us
  starting transfers between devices: 3.65 us -> 0 us
    pallas_call x0 -> x1, Pallas kernels: none -> 104 us  [fused_device(): pl.pallas_call(functools.partial(fused_kernel, sizes), out_shape=jax.Shap...]
    dot_general x8 -> x0, matrix products: 67.7 us -> none  [the longest x2 45.9 us: layer_pass(): jnp.dot(normed_full, query_cols, preferred_element_type=jnp.float32)]
    all_to_all x1 -> x0, blocking collectives: 54.2 us -> none  [on_device(): lax.all_to_all(packed, 'dp', split_axis=0, concat_axis=0, tiled=True)]
    ppermute x2 -> x0, waiting for transfers between devices: 25.4 us -> none  [passed_along(): return lax.ppermute(block, axis, route)]
    all_gather x2 -> x0, waiting for transfers between devices: 21.2 us -> none  [layer_pass(): whole = lax.all_gather(current, 'tensor', axis=1, tiled=True)]
    reduce_sum x5 -> x0, other arithmetic: 4.77 us -> none  [the longest x2 4.45 us: layer_pass(): scale_row = lax.rsqrt(jnp.sum(whole_wide * whole_wide, axis=-1) / D + 1e-05)]
    all_gather x2 -> x0, blocking collectives: 4.54 us -> none  [attend_heads(): kv_whole = lax.all_gather(kv_local, 'tensor', axis=1, tiled=True)]
    reshape x2 -> x0, local copies, waits for them, and re-layouts: 3.93 us -> none  [attend_heads(): return attended.reshape(row_count, queries.shape[1])]
  transfers between devices with their start and end apart: 4 -> 0, of which waited for: 4 -> 0; matrix products, arithmetic and copies ran while one was open for 1% -> 0% of each run, Pallas kernels for 0% -> 0%
where the time goes in v1:
time: 110 us
  Pallas kernels  104 us (95%)
  local copies, waits for them, and re-layouts  5.68 us (5%)
    pallas_call x1, Pallas kernels, fused_device(): pl.pallas_call(functools.partial(fused_kernel, sizes), out_shape=jax.Shap...  104 us
    unnamed x1, local copies, waits for them, and re-layouts  3.13 us
    scatter x2, local copies, waits for them, and re-layouts, fused_device(): meta.at[0, :docs].set(doc_lengths[0, 0]).at[1, :docs].set(doc_target[0, 0])  2.55 us

profile of v1, /device:TPU:0, one launch (start us, length us, event | category | flops | bytes accessed | tf_op | source)
XLA Modules:
  0.0 109.6 jit_solution(10482493867954321211)
XLA Ops:
  0.0 1.3 %scatter.6 = s32[8,128]{1,0:T(8,128)} pad(s32[1,8]{1,0:T(1,128)} %bitcast.9, s32[]{:T(128)} %constant.53.clone.1), padding=0_7x0_120 | pad | bytes 4132 | tf_op jit(solution)/shard_map/scatter | solution.py:415
  1.3 1.3 %scatter.9.meta = s32[8,128]{1,0:T(8,128)} dynamic-update-slice(s32[8,128]{1,0:T(8,128)} %scatter.6, s32[1,8]{1,0:T(1,128)} %bitcast.10, s32[]{:T(128)} %constant.54.clone.1, s32[]{:T(128)} %constant.53.clone.1) | dynamic-update-slice | bytes 68 | tf_op jit(solution)/shard_map/scatter | solution.py:415
  2.5 103.9 %shard_map.64 = bf16[256,4096]{1,0:T(8,128)(2,1)} custom-call(bf16[128,4096]{1,0:T(8,128)(2,1)} %bitcast.8, s32[8,128]{1,0:T(8,128)} %scatter.9.meta, f32[1,8192]{1,0:T(1,128)} %gain.1, bf16[8192,4096]{1,0:T(8,128)(2,1)} %bitcast.3.wq, bf16[8192,1024]{1,0:T(8,128)(2,1)} %bitcast.6), custom_call_target="tpu_custom_call" | custom-call | tf_op jit(solution)/shard_map/pallas_call | solution.py:420
  106.4 3.1 %copy.9 = bf16[1,256,4096]{2,1,0:T(8,128)(2,1)} copy(bf16[1,256,4096]{2,1,0:T(8,128)(2,1)} %bitcast.7) | data formatting | bytes 4194304

commit v2 on v1

--- a/solution.py
+++ b/solution.py
@@ -108,10 +108,13 @@
 
 def fused_kernel(
     sizes, hidden, meta, gain, wq, wkv, out,
-    x_own, x_other, h_send, next_own, next_other, meta_next, normed, spread, kv_cols,
-    kv_send, kv_heads, kv_weights, ring, mask, chooser, q_held, packed,
+    x_own, x_other, h_send, next_own, next_other, early_own, early_other, early_send,
+    meta_next, meta_early, normed, spread, kv_cols,
+    kv_send, kv_heads, kv_weights, ring, mask, early_mask, valid, early_chooser, late_chooser,
+    q_held, packed, early_out,
     sem_x, sem_xs, sem_xr, sem_ms, sem_mr, sem_kvw, sem_ring, sem_kvs, sem_kvr,
     sem_hs, sem_hr, sem_fs, sem_fr, sem_as, sem_ar, sem_own,
+    sem_es, sem_er, sem_gs, sem_gr, sem_mes, sem_mer,
 ):
     n_dp, n_pipe, docs = sizes
     rows, width = hidden.shape
@@ -121,7 +124,8 @@
     own_kv = kv_heads.shape[2]
     chunk_heads = CHUNK // HD
     group_chunks = n_chunks // own_kv
-    capacity = packed.shape[1]
+    half, capacity = packed.shape[:2]
+    early_rows = half * capacity
     dp = lax.axis_index("dp")
     pipe = lax.axis_index("pipe")
     side = lax.axis_index("tensor")
@@ -129,6 +133,9 @@
     following = lax.rem(pipe + 1, n_pipe)
     preceding = lax.rem(pipe + n_pipe - 1, n_pipe)
     total = STEPS * n_chunks
+    layer_rows = (rows, rows + early_rows)
+    parity = lax.rem(dp, 2)
+    slot_own = dp // 2
 
     def cols(j):
         return pl.ds(pl.multiple_of(j * CHUNK, CHUNK), CHUNK)
@@ -157,9 +164,49 @@
             device_id={"pipe": following}, device_id_type=pl.DeviceIdType.MESH,
         )
 
+    def meta_on(k):
+        return pltpu.make_async_remote_copy(
+            meta_next, meta_early.at[slot_own], sem_mes.at[k], sem_mer.at[k],
+            device_id={"dp": lax.rem(dp + 2 * k, n_dp)}, device_id_type=pl.DeviceIdType.MESH,
+        )
+
+    def meta_in(k):
+        source = lax.rem(dp + n_dp - 2 * k, n_dp)
+        return pltpu.make_async_remote_copy(
+            meta_next, meta_early.at[source // 2], sem_mes.at[k], sem_mer.at[k],
+            device_id={"dp": lax.rem(dp + 2 * k, n_dp)}, device_id_type=pl.DeviceIdType.MESH,
+        )
+
+    def slot_rows(slot):
+        return pl.ds(pl.multiple_of(slot * capacity, capacity), capacity)
+
+    def early_remote(k, j):
+        target = lax.rem(dp + 2 * k, n_dp)
+        return pltpu.make_async_remote_copy(
+            early_send.at[j, target // 2], early_own.at[j, slot_rows(slot_own)],
+            sem_es.at[k, j], sem_er.at[k, j],
+            device_id={"dp": target}, device_id_type=pl.DeviceIdType.MESH,
+        )
+
+    def early_in(k, j):
+        target = lax.rem(dp + 2 * k, n_dp)
+        source = lax.rem(dp + n_dp - 2 * k, n_dp)
+        return pltpu.make_async_remote_copy(
+            early_send.at[j, target // 2], early_own.at[j, slot_rows(source // 2)],
+            sem_es.at[k, j], sem_er.at[k, j],
+            device_id={"dp": target}, device_id_type=pl.DeviceIdType.MESH,
+        )
+
+    def early_forward(j):
+        return pltpu.make_async_remote_copy(
+            early_own.at[j], early_other.at[j], sem_gs.at[j], sem_gr.at[j],
+            device_id={"tensor": other}, device_id_type=pl.DeviceIdType.MESH,
+        )
+
     def kv_remote(layer):
-        return pltpu.make_async_remote_copy(
-            kv_send.at[layer], kv_heads.at[layer, side], sem_kvs.at[layer], sem_kvr.at[layer],
+        here = pl.ds(0, layer_rows[layer])
+        return pltpu.make_async_remote_copy(
+            kv_send.at[layer, :, here], kv_heads.at[layer, side, :, here], sem_kvs.at[layer], sem_kvr.at[layer],
             device_id={"tensor": other}, device_id_type=pl.DeviceIdType.MESH,
         )
 
@@ -181,7 +228,7 @@
     def doc_remote(away, j):
         target = lax.rem(dp + away, n_dp)
         return pltpu.make_async_remote_copy(
-            packed.at[target, :, cols(j)], out.at[doc_rows(dp), cols(j)],
+            packed.at[target // 2, :, cols(j)], out.at[doc_rows(dp), cols(j)],
             sem_as.at[away], sem_ar.at[away],
             device_id={"dp": target}, device_id_type=pl.DeviceIdType.MESH,
         )
@@ -190,9 +237,20 @@
         target = lax.rem(dp + away, n_dp)
         source = lax.rem(dp + n_dp - away, n_dp)
         return pltpu.make_async_remote_copy(
-            packed.at[target], out.at[doc_rows(source)],
+            packed.at[target // 2], out.at[doc_rows(source)],
             sem_as.at[away], sem_ar.at[away],
             device_id={"dp": target}, device_id_type=pl.DeviceIdType.MESH,
+        )
+
+    def early_store(slot, j):
+        return pltpu.make_async_copy(
+            early_out.at[slot, :, cols(j)], out.at[doc_rows(2 * slot + parity), cols(j)],
+            sem_own.at[slot],
+        )
+
+    def early_stored(slot):
+        return pltpu.make_async_copy(
+            early_out.at[slot], out.at[doc_rows(2 * slot + parity)], sem_own.at[slot]
         )
 
     for j in range(n_chunks):
@@ -252,42 +310,70 @@
         for i in range(chunk_heads):
             mask[i * rows:(i + 1) * rows, :] = allowed
 
-    def fill_chooser(source):
+    def fill_early_mask():
+        row = lax.broadcasted_iota(jnp.int32, (early_rows, early_rows), 0)
+        col = lax.broadcasted_iota(jnp.int32, (early_rows, early_rows), 1)
+        allowed = jnp.where((row // capacity == col // capacity) & (row >= col), 1.0, 0.0)
+        for i in range(chunk_heads):
+            early_mask[i * early_rows:(i + 1) * early_rows, :] = allowed
+
+    def fill_valid():
+        row = lax.broadcasted_iota(jnp.int32, (capacity, CHUNK), 0)
+        for slot in range(half):
+            size = jnp.zeros((1, 1), jnp.int32)
+            for d in range(docs):
+                here = meta_early[slot, 1:2, d:d + 1] == dp
+                size = size + jnp.where(here, meta_early[slot, 0:1, d:d + 1], 0)
+            valid[slot * capacity:(slot + 1) * capacity, :] = jnp.where(row < size, 1.0, 0.0)
+
+    def fill_choosers(source):
         row = lax.broadcasted_iota(jnp.int32, (1, rows), 1)
-        goal = jnp.full((1, rows), -1, jnp.int32)
+        nowhere = jnp.full((1, rows), -1, jnp.int32)
+        goals = [nowhere, nowhere]
         begin = jnp.zeros((1, 1), jnp.int32)
         for d in range(docs):
             end = begin + source[0:1, d:d + 1]
-            place = source[1:2, d:d + 1] * capacity + row - begin
-            goal = jnp.where((row >= begin) & (row < end), place, goal)
+            target = source[1:2, d:d + 1]
+            place = (target // 2) * capacity + row - begin
+            inside = (row >= begin) & (row < end)
+            same = target % 2 == parity
+            goals = [
+                jnp.where(inside & same, place, goals[0]),
+                jnp.where(inside & ~same, place, goals[1]),
+            ]
             begin = end
-        slot = lax.broadcasted_iota(jnp.int32, (n_dp * capacity, rows), 0)
-        chooser[...] = (slot == goal).astype(jnp.float32).astype(jnp.bfloat16)
-
-    def normalise(mine, theirs):
+        slot = lax.broadcasted_iota(jnp.int32, (early_rows, rows), 0)
+        for ref, goal in zip((early_chooser, late_chooser), goals):
+            ref[...] = (slot == goal).astype(jnp.float32).astype(jnp.bfloat16)
+
+    def normalise(mine, theirs, first, count):
+        held_rows = pl.ds(first, count)
+
         def squares(j, acc):
             a = mine[j].astype(jnp.float32)
             b = theirs[j].astype(jnp.float32)
             return acc + a * a + b * b
 
-        acc = lax.fori_loop(0, n_chunks, squares, jnp.zeros((rows, CHUNK), jnp.float32))
+        acc = lax.fori_loop(0, n_chunks, squares, jnp.zeros((count, CHUNK), jnp.float32))
         scale = lax.rsqrt(jnp.sum(acc, axis=-1, keepdims=True) / features + 1e-05)
 
         def write(j, carry):
             for held, half in ((mine, side), (theirs, other)):
                 where = cols(half * n_chunks + j)
                 wide = held[j].astype(jnp.float32) * scale * gain[:, where]
-                normed[:, where] = wide.astype(jnp.bfloat16)
+                normed[held_rows, where] = wide.astype(jnp.bfloat16)
             return carry
 
         lax.fori_loop(0, n_chunks, write, 0)
 
     def keys_values(layer):
+        count = layer_rows[layer]
+
         def one(n, carry):
             if layer == 0:
                 kv_copy(n).wait()
-            kv_cols[:, cols(n)] = jnp.dot(
-                normed[...], kv_weights[n], preferred_element_type=jnp.float32
+            kv_cols[0:count, cols(n)] = jnp.dot(
+                normed[0:count, :], kv_weights[n], preferred_element_type=jnp.float32
             ).astype(jnp.bfloat16)
             return carry
 
@@ -295,68 +381,91 @@
         for which, keep in ((other, False), (side, True)):
             first = pl.multiple_of(which * own_kv * HD, own_kv * HD)
             heads = jnp.dot(
-                kv_cols[...], spread[:, pl.ds(first, own_kv * HD)],
+                kv_cols[0:count, :], spread[:, pl.ds(first, own_kv * HD)],
                 preferred_element_type=jnp.float32,
             ).astype(jnp.bfloat16)
             for g in range(own_kv):
                 if keep:
-                    kv_heads[layer, side, g] = heads[:, g * HD:(g + 1) * HD]
+                    kv_heads[layer, side, g, 0:count] = heads[:, g * HD:(g + 1) * HD]
                 else:
-                    kv_send[layer, g] = heads[:, g * HD:(g + 1) * HD]
+                    kv_send[layer, g, 0:count] = heads[:, g * HD:(g + 1) * HD]
             if not keep:
                 kv_remote(layer).start()
 
-    def query(c):
+    def query(layer, c):
         return jnp.dot(
-            normed[...], ring[lax.rem(c, SLOTS)], preferred_element_type=jnp.float32
+            normed[0:layer_rows[layer], :], ring[lax.rem(c, SLOTS)], preferred_element_type=jnp.float32
         ).astype(jnp.bfloat16)
 
-    def attend(layer, j, mine):
-        q = q_held[lax.rem(j, 2)]
+    def attend(layer, j, mine, first, count, allowed):
+        here = slice(first, first + count)
+        q = q_held[lax.rem(j, 2), here]
         g = j // group_chunks
         stacked = jnp.concatenate([q[:, i * HD:(i + 1) * HD] for i in range(chunk_heads)], axis=0)
         scores = lax.dot_general(
-            stacked, kv_heads[layer, 0, g], (((1,), (1,)), ((), ())),
+            stacked, kv_heads[layer, 0, g, here], (((1,), (1,)), ((), ())),
             preferred_element_type=jnp.float32,
         ) * HD ** (-0.5)
-        e = jnp.where(mask[...] > 0.0, jnp.exp(scores), 0.0)
+        e = jnp.where(allowed[...] > 0.0, jnp.exp(scores), 0.0)
         p = (e * (1.0 / jnp.sum(e, axis=-1, keepdims=True))).astype(jnp.bfloat16)
-        a = jnp.dot(p, kv_heads[layer, 1, g], preferred_element_type=jnp.float32)
+        a = jnp.dot(p, kv_heads[layer, 1, g, here], preferred_element_type=jnp.float32)
         side_by_side = jnp.concatenate(
-            [a[i * rows:(i + 1) * rows] for i in range(chunk_heads)], axis=1
+            [a[i * count:(i + 1) * count] for i in range(chunk_heads)], axis=1
         )
         return (mine[j].astype(jnp.float32) + side_by_side).astype(jnp.bfloat16)
+
+    def attend_all(layer, j):
+        if layer == 0:
+            return (attend(0, j, x_own, 0, rows, mask),)
+        return (
+            attend(1, j, next_own, 0, rows, mask),
+            attend(1, j, early_own, rows, early_rows, early_mask),
+        )
 
     def refill(c):
         @pl.when(c + SLOTS < total)
         def _():
             ring_copy(c + SLOTS).start()
 
-    def run_layer(layer, mine, finish):
+    def run_layer(layer, finish):
+        count = layer_rows[layer]
         base = layer * n_chunks
         ring_copy(base).wait()
-        q_held[0] = query(base)
+        q_held[0, 0:count] = query(layer, base)
         refill(jnp.int32(base))
         kv_remote(layer).wait()
 
         def one(j, carry):
             c = base + j
             ring_copy(c).wait()
-            fresh = query(c)
-            done = attend(layer, j - 1, mine)
-            q_held[lax.rem(j, 2)] = fresh
+            fresh = query(layer, c)
+            done = attend_all(layer, j - 1)
+            q_held[lax.rem(j, 2), 0:count] = fresh
             refill(c)
-            finish(j - 1, done)
+            finish(j - 1, *done)
             return carry
 
         lax.fori_loop(1, n_chunks, one, 0)
-        finish(n_chunks - 1, attend(layer, n_chunks - 1, mine))
-
-    lag = 4
+        finish(n_chunks - 1, *attend_all(layer, n_chunks - 1))
+
+    lag, early_lag = 4, 7
 
     def pass_on(j):
         h_remote(j).wait_recv()
         forward_remote(j).start()
+        picked = jnp.dot(
+            early_chooser[...], next_own[j], preferred_element_type=jnp.float32
+        ).astype(jnp.bfloat16)
+        for slot in range(half):
+            early_send[j, slot] = picked[slot * capacity:(slot + 1) * capacity]
+        for k in range(1, half):
+            early_remote(k, j).start()
+        early_own[j, slot_rows(slot_own)] = early_send[j, slot_own]
+
+    def pass_early(j):
+        for k in range(1, half):
+            early_in(k, j).wait_recv()
+        early_forward(j).start()
 
     def send_next(j, done):
         h_send[j] = done
@@ -366,38 +475,60 @@
         def _():
             pass_on(j - lag)
 
-    def send_docs(j, done):
-        picked = jnp.dot(chooser[...], done, preferred_element_type=jnp.float32)
+        @pl.when(j >= early_lag)
+        def _():
+            pass_early(j - early_lag)
+
+    def send_docs(j, done, early):
+        picked = jnp.dot(late_chooser[...], done, preferred_element_type=jnp.float32)
         picked = picked.astype(jnp.bfloat16)
-        for i in range(n_dp):
-            packed[i, :, cols(j)] = picked[i * capacity:(i + 1) * capacity]
-        for away in range(1, n_dp):
+        kept = jnp.where(valid[...] > 0.0, early.astype(jnp.float32), 0.0).astype(jnp.bfloat16)
+        for slot in range(half):
+            here = slice(slot * capacity, (slot + 1) * capacity)
+            packed[slot, :, cols(j)] = picked[here]
+            early_out[slot, :, cols(j)] = kept[here]
+        for away in range(1, n_dp, 2):
             doc_remote(away, j).start()
+        for slot in range(half):
+            early_store(slot, j).start()
 
     fill_mask(meta)
+    fill_early_mask()
+    meta_remote().wait()
+    for k in range(1, half):
+        meta_on(k).start()
+    meta_early[slot_own] = meta_next[...]
+    fill_choosers(meta_next)
     for j in range(n_chunks):
         x_copy(j).wait()
     for j in range(n_chunks):
         x_remote(j).wait()
-    normalise(x_own, x_other)
+    normalise(x_own, x_other, 0, rows)
     keys_values(0)
-    run_layer(0, x_own, send_next)
+    run_layer(0, send_next)
     for j in range(n_chunks - lag, n_chunks):
         pass_on(j)
-    meta_remote().wait()
     fill_mask(meta_next)
-    fill_chooser(meta_next)
+    for k in range(1, half):
+        meta_in(k).wait()
+    fill_valid()
+    for j in range(n_chunks - early_lag, n_chunks):
+        pass_early(j)
     for j in range(n_chunks):
         forward_remote(j).wait()
-    normalise(next_own, next_other)
+    normalise(next_own, next_other, 0, rows)
+    for j in range(n_chunks):
+        early_forward(j).wait()
+    normalise(early_own, early_other, rows, early_rows)
     keys_values(1)
-    run_layer(1, next_own, send_docs)
-    mine = pltpu.make_async_copy(packed.at[dp], out.at[doc_rows(dp)], sem_own)
-    mine.start()
+    run_layer(1, send_docs)
     for j in range(n_chunks):
         h_remote(j).wait_send()
-    mine.wait()
-    for away in range(1, n_dp):
+        for k in range(1, half):
+            early_remote(k, j).wait_send()
+    for slot in range(half):
+        early_stored(slot).wait()
+    for away in range(1, n_dp, 2):
         doc_all(away).wait()
 
 
@@ -416,7 +547,11 @@
     bf16 = jnp.bfloat16
     dma = pltpu.SemaphoreType.DMA
     vmem = pltpu.VMEM
+    half = n_dp // 2
+    early_rows = half * capacity
+    most = rows + early_rows
     blocks = vmem((n_chunks, rows, CHUNK), bf16)
+    early_blocks = vmem((n_chunks, early_rows, CHUNK), bf16)
     result = pl.pallas_call(
         functools.partial(fused_kernel, sizes),
         out_shape=jax.ShapeDtypeStruct((n_dp * capacity, width), bf16),
@@ -429,26 +564,34 @@
         ],
         out_specs=pl.BlockSpec(memory_space=pl.ANY),
         scratch_shapes=[
-            blocks, blocks, blocks, blocks, blocks,
+            blocks, blocks, blocks, blocks, blocks, early_blocks, early_blocks,
+            vmem((n_chunks, half, capacity, CHUNK), bf16),
             vmem((8, 128), jnp.int32),
-            vmem((rows, features), bf16),
+            vmem((half, 8, 128), jnp.int32),
+            vmem((most, features), bf16),
             vmem((n_kv, n_kv), bf16),
-            vmem((rows, n_kv), bf16),
-            vmem((STEPS, own_kv, rows, HD), bf16),
-            vmem((STEPS, 2, own_kv, rows, HD), bf16),
+            vmem((most, n_kv), bf16),
+            vmem((STEPS, own_kv, most, HD), bf16),
+            vmem((STEPS, 2, own_kv, most, HD), bf16),
             vmem((kv_chunks, features, CHUNK), bf16),
             vmem((SLOTS, features, CHUNK), bf16),
             vmem((chunk_heads * rows, rows), jnp.float32),
-            vmem((n_dp * capacity, rows), bf16),
-            vmem((2, rows, CHUNK), bf16),
-            vmem((n_dp, capacity, width), bf16),
+            vmem((chunk_heads * early_rows, early_rows), jnp.float32),
+            vmem((early_rows, CHUNK), jnp.float32),
+            vmem((early_rows, rows), bf16),
+            vmem((early_rows, rows), bf16),
+            vmem((2, most, CHUNK), bf16),
+            vmem((half, capacity, width), bf16),
+            vmem((half, capacity, width), bf16),
             dma((n_chunks,)), dma((n_chunks,)), dma((n_chunks,)), dma, dma,
             dma((kv_chunks,)), dma((SLOTS,)), dma((STEPS,)), dma((STEPS,)),
             dma((n_chunks,)), dma((n_chunks,)), dma((n_chunks,)), dma((n_chunks,)),
-            dma((n_dp,)), dma((n_dp,)), dma,
+            dma((n_dp,)), dma((n_dp,)), dma((half,)),
+            dma((half, n_chunks)), dma((half, n_chunks)), dma((n_chunks,)), dma((n_chunks,)),
+            dma((half,)), dma((half,)),
         ],
         compiler_params=pltpu.CompilerParams(
-            collective_id=0, has_side_effects=True, vmem_limit_bytes=66 * 1024 * 1000
+            collective_id=0, has_side_effects=True, vmem_limit_bytes=67043328
         ),
     )(hidden[0], meta, norm_gain, q_weight[0], kv_weight[0])
     return result[None]
@@ -464,7 +607,7 @@
         P("pipe", None, "tensor"),
     )
     run = on_device
-    if mesh.shape["tensor"] == 2:
+    if mesh.shape["tensor"] == 2 and mesh.shape["dp"] % 2 == 0:
         sizes = (mesh.shape["dp"], mesh.shape["pipe"], mesh.shape["dp"])
         run = functools.partial(fused_device, sizes)
     return jax.shard_map(

time: 110 us -> 102 us (0.927)
  Pallas kernels: 104 us -> 96.5 us
    pallas_call x1, Pallas kernels: 104 us -> 96.5 us  [fused_device(): pl.pallas_call(functools.partial(fused_kernel, sizes), out_shape=jax.Shap...]
where the time goes in v2:
time: 102 us
  Pallas kernels  96.5 us (95%)
  local copies, waits for them, and re-layouts  5.68 us (6%)
    pallas_call x1, Pallas kernels, fused_device(): pl.pallas_call(functools.partial(fused_kernel, sizes), out_shape=jax.Shap...  96.5 us
    unnamed x1, local copies, waits for them, and re-layouts  3.13 us
    scatter x2, local copies, waits for them, and re-layouts, fused_device(): meta.at[0, :docs].set(doc_lengths[0, 0]).at[1, :docs].set(doc_target[0, 0])  2.55 us

profile of v2, /device:TPU:0, one launch (start us, length us, event | category | flops | bytes accessed | tf_op | source)
XLA Modules:
  0.0 102.2 jit_solution(4072329778779249836)
XLA Ops:
  0.0 1.3 %scatter.6 = s32[8,128]{1,0:T(8,128)} pad(s32[1,8]{1,0:T(1,128)} %bitcast.9, s32[]{:T(128)} %constant.53.clone.1), padding=0_7x0_120 | pad | bytes 4132 | tf_op jit(solution)/shard_map/scatter | solution.py:546
  1.3 1.3 %scatter.9.meta = s32[8,128]{1,0:T(8,128)} dynamic-update-slice(s32[8,128]{1,0:T(8,128)} %scatter.6, s32[1,8]{1,0:T(1,128)} %bitcast.10, s32[]{:T(128)} %constant.54.clone.1, s32[]{:T(128)} %constant.53.clone.1) | dynamic-update-slice | bytes 68 | tf_op jit(solution)/shard_map/scatter | solution.py:546
  2.5 96.5 %shard_map.64 = bf16[256,4096]{1,0:T(8,128)(2,1)} custom-call(bf16[128,4096]{1,0:T(8,128)(2,1)} %bitcast.8, s32[8,128]{1,0:T(8,128)} %scatter.9.meta, f32[1,8192]{1,0:T(1,128)} %gain.1, bf16[8192,4096]{1,0:T(8,128)(2,1)} %bitcast.3.wq, bf16[8192,1024]{1,0:T(8,128)(2,1)} %bitcast.6), custom_call_target="tpu_custom_call" | custom-call | tf_op jit(solution)/shard_map/pallas_call | solution.py:555
  99.1 3.1 %copy.9 = bf16[1,256,4096]{2,1,0:T(8,128)(2,1)} copy(bf16[1,256,4096]{2,1,0:T(8,128)(2,1)} %bitcast.7) | data formatting | bytes 4194304

commit v3 on v2

--- a/solution.py
+++ b/solution.py
@@ -106,8 +106,13 @@
 SLOTS = 6
 
 
+def split_masks(n_dp):
+    early = [m for m in range(n_dp) if m >= n_dp // 2 and m % 2 == 0]
+    return early, [m for m in range(n_dp) if m not in early]
+
+
 def fused_kernel(
-    sizes, hidden, meta, gain, wq, wkv, out,
+    sizes, hidden, lengths, targets, gain, wq, wkv, out, meta,
     x_own, x_other, h_send, next_own, next_other, early_own, early_other, early_send,
     meta_next, meta_early, normed, spread, kv_cols,
     kv_send, kv_heads, kv_weights, ring, mask, early_mask, valid, early_chooser, late_chooser,
@@ -124,7 +129,9 @@
     own_kv = kv_heads.shape[2]
     chunk_heads = CHUNK // HD
     group_chunks = n_chunks // own_kv
-    half, capacity = packed.shape[:2]
+    capacity = packed.shape[1]
+    early_masks, late_masks = split_masks(n_dp)
+    half = len(early_masks)
     early_rows = half * capacity
     dp = lax.axis_index("dp")
     pipe = lax.axis_index("pipe")
@@ -134,8 +141,17 @@
     preceding = lax.rem(pipe + n_pipe - 1, n_pipe)
     total = STEPS * n_chunks
     layer_rows = (rows, rows + early_rows)
-    parity = lax.rem(dp, 2)
-    slot_own = dp // 2
+
+    def partner(flips):
+        index, bit = dp, 1
+        while bit < n_dp:
+            if flips & bit:
+                index = index + bit - 2 * bit * lax.rem(dp // bit, 2)
+            bit *= 2
+        return index
+
+    early_partners = [partner(m) for m in early_masks]
+    late_partners = [partner(m) for m in late_masks]
 
     def cols(j):
         return pl.ds(pl.multiple_of(j * CHUNK, CHUNK), CHUNK)
@@ -166,35 +182,15 @@
 
     def meta_on(k):
         return pltpu.make_async_remote_copy(
-            meta_next, meta_early.at[slot_own], sem_mes.at[k], sem_mer.at[k],
-            device_id={"dp": lax.rem(dp + 2 * k, n_dp)}, device_id_type=pl.DeviceIdType.MESH,
-        )
-
-    def meta_in(k):
-        source = lax.rem(dp + n_dp - 2 * k, n_dp)
-        return pltpu.make_async_remote_copy(
-            meta_next, meta_early.at[source // 2], sem_mes.at[k], sem_mer.at[k],
-            device_id={"dp": lax.rem(dp + 2 * k, n_dp)}, device_id_type=pl.DeviceIdType.MESH,
-        )
-
-    def slot_rows(slot):
-        return pl.ds(pl.multiple_of(slot * capacity, capacity), capacity)
+            meta_next, meta_early.at[k], sem_mes.at[k], sem_mer.at[k],
+            device_id={"dp": early_partners[k]}, device_id_type=pl.DeviceIdType.MESH,
+        )
 
     def early_remote(k, j):
-        target = lax.rem(dp + 2 * k, n_dp)
-        return pltpu.make_async_remote_copy(
-            early_send.at[j, target // 2], early_own.at[j, slot_rows(slot_own)],
+        return pltpu.make_async_remote_copy(
+            early_send.at[j, k], early_own.at[j, k * capacity:(k + 1) * capacity],
             sem_es.at[k, j], sem_er.at[k, j],
-            device_id={"dp": target}, device_id_type=pl.DeviceIdType.MESH,
-        )
-
-    def early_in(k, j):
-        target = lax.rem(dp + 2 * k, n_dp)
-        source = lax.rem(dp + n_dp - 2 * k, n_dp)
-        return pltpu.make_async_remote_copy(
-            early_send.at[j, target // 2], early_own.at[j, slot_rows(source // 2)],
-            sem_es.at[k, j], sem_er.at[k, j],
-            device_id={"dp": target}, device_id_type=pl.DeviceIdType.MESH,
+            device_id={"dp": early_partners[k]}, device_id_type=pl.DeviceIdType.MESH,
         )
 
     def early_forward(j):
@@ -225,32 +221,37 @@
     def doc_rows(index):
         return pl.ds(pl.multiple_of(index * capacity, capacity), capacity)
 
-    def doc_remote(away, j):
-        target = lax.rem(dp + away, n_dp)
-        return pltpu.make_async_remote_copy(
-            packed.at[target // 2, :, cols(j)], out.at[doc_rows(dp), cols(j)],
-            sem_as.at[away], sem_ar.at[away],
-            device_id={"dp": target}, device_id_type=pl.DeviceIdType.MESH,
-        )
-
-    def doc_all(away):
-        target = lax.rem(dp + away, n_dp)
-        source = lax.rem(dp + n_dp - away, n_dp)
-        return pltpu.make_async_remote_copy(
-            packed.at[target // 2], out.at[doc_rows(source)],
-            sem_as.at[away], sem_ar.at[away],
-            device_id={"dp": target}, device_id_type=pl.DeviceIdType.MESH,
-        )
-
-    def early_store(slot, j):
+    def doc_remote(k, j):
+        return pltpu.make_async_remote_copy(
+            packed.at[k, :, cols(j)], out.at[doc_rows(dp), cols(j)],
+            sem_as.at[k], sem_ar.at[k],
+            device_id={"dp": late_partners[k]}, device_id_type=pl.DeviceIdType.MESH,
+        )
+
+    def doc_all(k):
+        return pltpu.make_async_remote_copy(
+            packed.at[k], out.at[doc_rows(late_partners[k])],
+            sem_as.at[k], sem_ar.at[k],
+            device_id={"dp": late_partners[k]}, device_id_type=pl.DeviceIdType.MESH,
+        )
+
+    def own_store(j):
         return pltpu.make_async_copy(
-            early_out.at[slot, :, cols(j)], out.at[doc_rows(2 * slot + parity), cols(j)],
-            sem_own.at[slot],
-        )
-
-    def early_stored(slot):
+            packed.at[0, :, cols(j)], out.at[doc_rows(dp), cols(j)], sem_own.at[half]
+        )
+
+    def own_stored():
+        return pltpu.make_async_copy(packed.at[0], out.at[doc_rows(dp)], sem_own.at[half])
+
+    def early_store(k, j):
         return pltpu.make_async_copy(
-            early_out.at[slot], out.at[doc_rows(2 * slot + parity)], sem_own.at[slot]
+            early_out.at[k, :, cols(j)], out.at[doc_rows(early_partners[k]), cols(j)],
+            sem_own.at[k],
+        )
+
+    def early_stored(k):
+        return pltpu.make_async_copy(
+            early_out.at[k], out.at[doc_rows(early_partners[k])], sem_own.at[k]
         )
 
     for j in range(n_chunks):
@@ -260,6 +261,9 @@
     for c in range(SLOTS):
         ring_copy(c).start()
 
+    meta[...] = jnp.zeros(meta.shape, jnp.int32)
+    meta[0:1, 0:docs] = lengths[...]
+    meta[1:2, 0:docs] = targets[...]
     barrier = pltpu.get_barrier_semaphore()
     pl.semaphore_signal(
         barrier, inc=1, device_id={"tensor": other}, device_id_type=pl.DeviceIdType.MESH
@@ -328,22 +332,20 @@
 
     def fill_choosers(source):
         row = lax.broadcasted_iota(jnp.int32, (1, rows), 1)
-        nowhere = jnp.full((1, rows), -1, jnp.int32)
-        goals = [nowhere, nowhere]
+        goals = [jnp.full((1, rows), -1, jnp.int32) for _ in range(2)]
         begin = jnp.zeros((1, 1), jnp.int32)
         for d in range(docs):
             end = begin + source[0:1, d:d + 1]
             target = source[1:2, d:d + 1]
-            place = (target // 2) * capacity + row - begin
             inside = (row >= begin) & (row < end)
-            same = target % 2 == parity
-            goals = [
-                jnp.where(inside & same, place, goals[0]),
-                jnp.where(inside & ~same, place, goals[1]),
-            ]
+            for i, partners in enumerate((early_partners, late_partners)):
+                first = jnp.full((1, 1), -n_dp * capacity, jnp.int32)
+                for k, index in enumerate(partners):
+                    first = jnp.where(target == index, k * capacity, first)
+                goals[i] = jnp.where(inside, first + row - begin, goals[i])
             begin = end
-        slot = lax.broadcasted_iota(jnp.int32, (early_rows, rows), 0)
         for ref, goal in zip((early_chooser, late_chooser), goals):
+            slot = lax.broadcasted_iota(jnp.int32, ref.shape, 0)
             ref[...] = (slot == goal).astype(jnp.float32).astype(jnp.bfloat16)
 
     def normalise(mine, theirs, first, count):
@@ -458,13 +460,12 @@
         ).astype(jnp.bfloat16)
         for slot in range(half):
             early_send[j, slot] = picked[slot * capacity:(slot + 1) * capacity]
-        for k in range(1, half):
+        for k in range(half):
             early_remote(k, j).start()
-        early_own[j, slot_rows(slot_own)] = early_send[j, slot_own]
 
     def pass_early(j):
-        for k in range(1, half):
-            early_in(k, j).wait_recv()
+        for k in range(half):
+            early_remote(k, j).wait_recv()
         early_forward(j).start()
 
     def send_next(j, done):
@@ -483,21 +484,21 @@
         picked = jnp.dot(late_chooser[...], done, preferred_element_type=jnp.float32)
         picked = picked.astype(jnp.bfloat16)
         kept = jnp.where(valid[...] > 0.0, early.astype(jnp.float32), 0.0).astype(jnp.bfloat16)
+        for slot in range(len(late_masks)):
+            packed[slot, :, cols(j)] = picked[slot * capacity:(slot + 1) * capacity]
+        for k in reversed(range(1, len(late_masks))):
+            doc_remote(k, j).start()
+        own_store(j).start()
         for slot in range(half):
-            here = slice(slot * capacity, (slot + 1) * capacity)
-            packed[slot, :, cols(j)] = picked[here]
-            early_out[slot, :, cols(j)] = kept[here]
-        for away in range(1, n_dp, 2):
-            doc_remote(away, j).start()
+            early_out[slot, :, cols(j)] = kept[slot * capacity:(slot + 1) * capacity]
         for slot in range(half):
             early_store(slot, j).start()
 
     fill_mask(meta)
     fill_early_mask()
     meta_remote().wait()
-    for k in range(1, half):
+    for k in range(half):
         meta_on(k).start()
-    meta_early[slot_own] = meta_next[...]
     fill_choosers(meta_next)
     for j in range(n_chunks):
         x_copy(j).wait()
@@ -509,8 +510,8 @@
     for j in range(n_chunks - lag, n_chunks):
         pass_on(j)
     fill_mask(meta_next)
-    for k in range(1, half):
-        meta_in(k).wait()
+    for k in range(half):
+        meta_on(k).wait()
     fill_valid()
     for j in range(n_chunks - early_lag, n_chunks):
         pass_early(j)
@@ -524,12 +525,13 @@
     run_layer(1, send_docs)
     for j in range(n_chunks):
         h_remote(j).wait_send()
-        for k in range(1, half):
+        for k in range(half):
             early_remote(k, j).wait_send()
     for slot in range(half):
         early_stored(slot).wait()
-    for away in range(1, n_dp, 2):
-        doc_all(away).wait()
+    own_stored().wait()
+    for k in range(1, len(late_masks)):
+        doc_all(k).wait()
 
 
 def fused_device(sizes, hidden, doc_lengths, doc_target, norm_gain, q_weight, kv_weight):
@@ -542,12 +544,11 @@
     own_kv = KV_HEADS // 2
     capacity = rows // 4
     chunk_heads = CHUNK // HD
-    meta = jnp.zeros((8, 128), jnp.int32)
-    meta = meta.at[0, :docs].set(doc_lengths[0, 0]).at[1, :docs].set(doc_target[0, 0])
     bf16 = jnp.bfloat16
     dma = pltpu.SemaphoreType.DMA
     vmem = pltpu.VMEM
-    half = n_dp // 2
+    early_masks, late_masks = split_masks(n_dp)
+    half, n_late = len(early_masks), len(late_masks)
     early_rows = half * capacity
     most = rows + early_rows
     blocks = vmem((n_chunks, rows, CHUNK), bf16)
@@ -559,11 +560,13 @@
             pl.BlockSpec(memory_space=pl.ANY),
             pl.BlockSpec(memory_space=pltpu.VMEM),
             pl.BlockSpec(memory_space=pltpu.VMEM),
+            pl.BlockSpec(memory_space=pltpu.VMEM),
             pl.BlockSpec(memory_space=pl.ANY),
             pl.BlockSpec(memory_space=pl.ANY),
         ],
         out_specs=pl.BlockSpec(memory_space=pl.ANY),
         scratch_shapes=[
+            vmem((8, 128), jnp.int32),
             blocks, blocks, blocks, blocks, blocks, early_blocks, early_blocks,
             vmem((n_chunks, half, capacity, CHUNK), bf16),
             vmem((8, 128), jnp.int32),
@@ -579,21 +582,21 @@
             vmem((chunk_heads * early_rows, early_rows), jnp.float32),
             vmem((early_rows, CHUNK), jnp.float32),
             vmem((early_rows, rows), bf16),
-            vmem((early_rows, rows), bf16),
+            vmem((n_late * capacity, rows), bf16),
             vmem((2, most, CHUNK), bf16),
-            vmem((half, capacity, width), bf16),
+            vmem((n_late, capacity, width), bf16),
             vmem((half, capacity, width), bf16),
             dma((n_chunks,)), dma((n_chunks,)), dma((n_chunks,)), dma, dma,
             dma((kv_chunks,)), dma((SLOTS,)), dma((STEPS,)), dma((STEPS,)),
             dma((n_chunks,)), dma((n_chunks,)), dma((n_chunks,)), dma((n_chunks,)),
-            dma((n_dp,)), dma((n_dp,)), dma((half,)),
+            dma((n_late,)), dma((n_late,)), dma((half + 1,)),
             dma((half, n_chunks)), dma((half, n_chunks)), dma((n_chunks,)), dma((n_chunks,)),
             dma((half,)), dma((half,)),
         ],
         compiler_params=pltpu.CompilerParams(
             collective_id=0, has_side_effects=True, vmem_limit_bytes=67043328
         ),
-    )(hidden[0], meta, norm_gain, q_weight[0], kv_weight[0])
+    )(hidden[0], doc_lengths[0], doc_target[0], norm_gain, q_weight[0], kv_weight[0])
     return result[None]
 
 
@@ -607,7 +610,7 @@
         P("pipe", None, "tensor"),
     )
     run = on_device
-    if mesh.shape["tensor"] == 2 and mesh.shape["dp"] % 2 == 0:
+    if mesh.shape["tensor"] == 2 and mesh.shape["dp"] in (4, 8, 16):
         sizes = (mesh.shape["dp"], mesh.shape["pipe"], mesh.shape["dp"])
         run = functools.partial(fused_device, sizes)
     return jax.shard_map(

time: 102 us -> 91.9 us (0.901)
  Pallas kernels: 96.5 us -> 88.6 us
  local copies, waits for them, and re-layouts: 5.68 us -> 3.13 us
    pallas_call x1, Pallas kernels: 96.5 us -> 88.6 us  [fused_device(): pl.pallas_call(functools.partial(fused_kernel, sizes), out_shape=jax.Shap...]
    scatter x2 -> x0, local copies, waits for them, and re-layouts: 2.55 us -> none  [fused_device(): meta.at[0, :docs].set(doc_lengths[0, 0]).at[1, :docs].set(doc_target[0, 0])]
where the time goes in v3:
time: 91.9 us; the launch traced here: 91.7 us
  Pallas kernels  88.6 us (96%)
  local copies, waits for them, and re-layouts  3.13 us (3%)
    pallas_call x1, Pallas kernels, fused_device(): pl.pallas_call(functools.partial(fused_kernel, sizes), out_shape=jax.Shap...  88.6 us
    unnamed x1, local copies, waits for them, and re-layouts  3.13 us

profile of v3, /device:TPU:0, one launch (start us, length us, event | category | flops | bytes accessed | tf_op | source)
XLA Modules:
  0.0 91.7 jit_solution(1747085036677919481)
XLA Ops:
  0.0 88.6 %shard_map.64 = bf16[256,4096]{1,0:T(8,128)(2,1)} custom-call(bf16[128,4096]{1,0:T(8,128)(2,1)} %bitcast.8, s32[1,8]{1,0:T(1,128)} %bitcast.9, s32[1,8]{1,0:T(1,128)} %bitcast.10, f32[1,8192]{1,0:T(1,128)} %gain.1, bf16[8192,4096]{1,0:T(8,128)(2,1)} %bitcast.3.wq, bf16[8192,1024]{1,0:T(8,128)(2,1)} %bitcast.6), custom_call_target="tpu_custom_call" | custom-call | tf_op jit(solution)/shard_map/pallas_call | solution.py:556
  88.6 3.1 %copy.8 = bf16[1,256,4096]{2,1,0:T(8,128)(2,1)} copy(bf16[1,256,4096]{2,1,0:T(8,128)(2,1)} %bitcast.7) | data formatting | bytes 4194304

commit v4 on v3

--- a/solution.py
+++ b/solution.py
@@ -170,7 +170,7 @@
 
     def x_remote(j):
         return pltpu.make_async_remote_copy(
-            hidden.at[:, cols(j)], x_other.at[j], sem_xs.at[j], sem_xr.at[j],
+            x_own.at[j], x_other.at[j], sem_xs.at[j], sem_xr.at[j],
             device_id={"tensor": other}, device_id_type=pl.DeviceIdType.MESH,
         )
 
@@ -283,9 +283,10 @@
             device_id_type=pl.DeviceIdType.MESH,
         )
     pl.semaphore_wait(barrier, greeted)
+    meta_remote().start()
     for j in range(n_chunks):
+        x_copy(j).wait()
         x_remote(j).start()
-    meta_remote().start()
 
     n_kv = kv_cols.shape[1]
     cols_wide = spread.shape[0]
@@ -500,8 +501,6 @@
     for k in range(half):
         meta_on(k).start()
     fill_choosers(meta_next)
-    for j in range(n_chunks):
-        x_copy(j).wait()
     for j in range(n_chunks):
         x_remote(j).wait()
     normalise(x_own, x_other, 0, rows)

time: 91.9 us -> 93.2 us (1.014)
  Pallas kernels: 88.6 us -> 89.8 us
    pallas_call x1, Pallas kernels: 88.6 us -> 89.8 us  [fused_device(): pl.pallas_call(functools.partial(fused_kernel, sizes), out_shape=jax.Shap...]
where the time goes in v4:
time: 93.2 us; the launch traced here: 92.9 us
  Pallas kernels  89.8 us (96%)
  local copies, waits for them, and re-layouts  3.13 us (3%)
    pallas_call x1, Pallas kernels, fused_device(): pl.pallas_call(functools.partial(fused_kernel, sizes), out_shape=jax.Shap...  89.8 us
    unnamed x1, local copies, waits for them, and re-layouts  3.13 us

profile of v4, /device:TPU:0, one launch (start us, length us, event | category | flops | bytes accessed | tf_op | source)
XLA Modules:
  0.0 92.9 jit_solution(3112101493947970035)
XLA Ops:
  0.0 89.8 %shard_map.64 = bf16[256,4096]{1,0:T(8,128)(2,1)} custom-call(bf16[128,4096]{1,0:T(8,128)(2,1)} %bitcast.8, s32[1,8]{1,0:T(1,128)} %bitcast.9, s32[1,8]{1,0:T(1,128)} %bitcast.10, f32[1,8192]{1,0:T(1,128)} %gain.1, bf16[8192,4096]{1,0:T(8,128)(2,1)} %bitcast.3.wq, bf16[8192,1024]{1,0:T(8,128)(2,1)} %bitcast.6), custom_call_target="tpu_custom_call" | custom-call | tf_op jit(solution)/shard_map/pallas_call | solution.py:555
  89.8 3.1 %copy.8 = bf16[1,256,4096]{2,1,0:T(8,128)(2,1)} copy(bf16[1,256,4096]{2,1,0:T(8,128)(2,1)} %bitcast.7) | data formatting | bytes 4194304
